TPU v7x, 128 devices: a whole 4x4x4 slice. The times are simulated.
128 devices in a mesh: sec: 2 (over z_lo), row: 8 (over x, z_hi), col: 8 (over y, core).
Axes of the slice: x: 4, y: 4, z: 4 (z_hi: 2, z_lo: 2; z = z_hi * 2 + z_lo), core: 2. Of those that a mesh axis runs over, the one named last changes fastest.
Arguments:
- held_inverse: bfloat16 [12288, 12288], P('row', ('sec', 'col')), as said below
- factor_panels: bfloat16 [2, 12288, 1024], P(None, ('sec', 'col'), 'row'), may hold values from -0.125 to 0.125
- block_inverses: bfloat16 [2, 1024, 1024], P(None, 'row'), as said below
- covariance: float32 [12288, 12288], P('row', ('sec', 'col')), may hold values from -0.9 to 0.9
Outputs:
- updated: float32 [12288, 12288], P('row', ('sec', 'col'))
Inputs may be any that keep to these rules, and one draw needn't show every extreme that they name: held_inverse is lower triangular with a positive diagonal. Each block of block_inverses is lower triangular with a positive diagonal.
All inputs are finite; a program needn't handle non-finite values.
Results may differ from a plain program's by a relative error of at most 0.0038.
Values may be sent and summed in bfloat16 or wider, within the bound.
A program may use at most 128 MiB of HBM per device.

v0:
```python
import jax
import jax.numpy as jnp
from jax import lax
from jax.sharding import Mesh
from jax.sharding import PartitionSpec as P

PANELS = 2
ROW = ("row_0", "row_1")


def scatter_axes(x, axes, dim):
    for axis in axes:
        x = lax.psum_scatter(x, axis, scatter_dimension=dim, tiled=True)
    return x


def from_root(x, axis, root):
    mine = lax.axis_index(axis) == root
    return lax.psum(jnp.where(mine, x, jnp.zeros_like(x)), axis)


def body(held_inverse, factor_panels, block_inverses, covariance):
    total = covariance
    tile_cols = held_inverse.shape[1]
    groups = lax.axis_size(("sec", "col"))
    ratio = groups // lax.axis_size(ROW)
    column_index = lax.axis_index(("sec", "col"))
    root_row = column_index // ratio
    offset = column_index % ratio * tile_cols
    for panel in range(PANELS):
        partial_value = jnp.dot(
            factor_panels[panel], block_inverses[panel], preferred_element_type=jnp.float32
        )
        scaled = scatter_axes(partial_value, ROW, 1).astype(jnp.bfloat16)
        terms = jnp.dot(
            held_inverse,
            lax.all_gather(scaled, ROW, axis=1, tiled=True),
            preferred_element_type=jnp.float32,
        )
        summed = lax.psum(terms, ("sec", "col"))
        inverse = (-summed).astype(jnp.bfloat16)
        own_block = lax.dynamic_slice_in_dim(inverse, offset, tile_cols, 0)
        column_block = from_root(own_block, ROW, root_row)
        total = total + lax.dot_general(
            inverse, column_block, (((1,), (1,)), ((), ())), preferred_element_type=jnp.float32
        )
    return total


def solution(mesh):
    split = Mesh(
        mesh.devices.reshape(mesh.shape["sec"], 4, 2, mesh.shape["col"]),
        ("sec", "row_0", "row_1", "col"),
    )
    in_specs = (
        P(ROW, ("sec", "col")),
        P(None, ("sec", "col"), ROW),
        P(None, ROW, None),
        P(ROW, ("sec", "col")),
    )
    out_specs = P(ROW, ("sec", "col"))
    return jax.shard_map(body, mesh=split, in_specs=in_specs, out_specs=out_specs, check_vma=False)
```

profile of v0, /device:TPU:5, one launch (start us, length us, event | category | flops | bytes accessed | tf_op | source)
XLA Modules:
  0.0 585.9 jit_solution(17937898365134801965)
XLA Ops:
  6.5 0.0 copy-start
  6.5 0.0 copy-start.4
  6.5 0.0 copy-start.5
  6.5 0.0 reduce-scatter.5.cloned.1.call-start
  6.5 3.4 fusion.2
  10.0 0.0 reduce-scatter.5.cloned.1.call-update
  10.0 0.0 reduce-scatter.9.cloned.1.call-start
  10.0 0.0 copy-done.4
  10.0 0.0 copy-done.5
  10.1 2.2 fusion
  12.3 0.0 reduce-scatter.9.cloned.1.call-update
  12.3 0.0 reduce-scatter.7.cloned.1.call-start
  12.3 36.8 %reduce-scatter.5.cloned.1.call-done = f32[768,256]{1,0:T(8,128)} async-done(((f32[768,1024]{1,0:T(8,128)}), f32[768,256]{1,0:T(8,128)}) %reduce-scatter.5.cloned.1.call-update) | async-done | bytes 786448 | tf_op jit(solution)/shard_map/reduce_scatter | solution.py:13
  49.2 0.0 reduce-scatter.7.cloned.1.call-update
  49.2 0.0 reduce-scatter.11.cloned.1.call-start
  49.2 40.3 %reduce-scatter.9.cloned.1.call-done = f32[768,256]{1,0:T(8,128)} async-done(((f32[768,1024]{1,0:T(8,128)}), f32[768,256]{1,0:T(8,128)}) %reduce-scatter.9.cloned.1.call-update) | async-done | bytes 786448 | tf_op jit(solution)/shard_map/reduce_scatter | solution.py:13
  89.6 0.0 reduce-scatter.11.cloned.1.call-update
  89.6 0.0 all-gather.3.cloned.1.call-start
  89.6 25.2 %reduce-scatter.7.cloned.1.call-done = f32[768,128]{1,0:T(8,128)} async-done(((f32[768,256]{1,0:T(8,128)}), f32[768,128]{1,0:T(8,128)}) %reduce-scatter.7.cloned.1.call-update) | async-done | bytes 393232 | tf_op jit(solution)/shard_map/reduce_scatter | solution.py:13
  114.8 1.7 convert_element_type.12
  116.5 0.0 all-gather.3.cloned.1.call-update
  116.6 0.0 all-gather.5.cloned.1.call-start
  116.6 21.3 %reduce-scatter.11.cloned.1.call-done = f32[768,128]{1,0:T(8,128)} async-done(((f32[768,256]{1,0:T(8,128)}), f32[768,128]{1,0:T(8,128)}) %reduce-scatter.11.cloned.1.call-update) | async-done | bytes 393232 | tf_op jit(solution)/shard_map/reduce_scatter | solution.py:13
  138.0 1.7 convert_element_type.14
  139.7 0.0 all-gather.5.cloned.1.call-update
  139.7 0.0 all-reduce.5.cloned.1.call-start
  139.7 49.3 %all-gather.3.cloned.1.call-done = bf16[768,1024]{1,0:T(8,128)(2,1)} async-done(((bf16[768,128]{1,0:T(8,128)(2,1)}), bf16[768,1024]{1,0:T(8,128)(2,1)}) %all-gather.3.cloned.1.call-update) | async-done | bytes 1572880 | tf_op jit(solution)/shard_map/all_gather | solution.py:37
  189.0 0.0 copy-done
  189.0 6.1 %convolution_bitcast_fusion.1 = f32[1536,1024]{0,1:T(8,128)} fusion(bf16[768,1024]{1,0:T(8,128)(2,1)} %all-gather.3.cloned.1.call-done, bf16[1536,768]{1,0:T(8,128)(2,1)S(1)} %copy-done), kind=kOutput, calls=%fused_computation.4 | convolution fusion | flops 2415919104 | bytes 10223616 | tf_op jit(solution)/shard_map/dot_general | solution.py:35
  195.2 47.0 %all-gather.5.cloned.1.call-done = bf16[768,1024]{1,0:T(8,128)(2,1)} async-done(((bf16[768,128]{1,0:T(8,128)(2,1)}), bf16[768,1024]{1,0:T(8,128)(2,1)}) %all-gather.5.cloned.1.call-update) | async-done | bytes 1572880 | tf_op jit(solution)/shard_map/all_gather | solution.py:37
  242.1 6.0 %convolution_bitcast_fusion = f32[1536,1024]{0,1:T(8,128)} fusion(bf16[768,1024]{1,0:T(8,128)(2,1)} %all-gather.5.cloned.1.call-done, bf16[1536,768]{1,0:T(8,128)(2,1)S(1)} %copy-done), kind=kOutput, calls=%fused_computation.3 | convolution fusion | flops 2415919104 | bytes 10223616 | tf_op jit(solution)/shard_map/dot_general | solution.py:35
  248.1 0.0 all-reduce.5.cloned.1.call-update
  248.1 0.0 all-reduce.7.cloned.1.call-start
  248.2 159.2 %all-reduce.5.cloned.1.call-done = (f32[1536,1024]{0,1:T(8,128)}, f32[1536,1024]{0,1:T(8,128)}) async-done(((f32[1536,1024]{0,1:T(8,128)}, f32[1536,1024]{0,1:T(8,128)}), (f32[1536,1024]{0,1:T(8,128)}, f32[1536,1024]{0,1:T(8,128)})) %all-reduce.5.cloned.1.call-update) | async-done | bytes 12582928 | tf_op jit(solution)/shard_map/psum | solution.py:40
  407.4 6.3 %negate_convert_fusion = (bf16[1536,1024]{0,1:T(8,128)(2,1)S(1)}, bf16[1536,1024]{0,1:T(8,128)(2,1)S(1)}) fusion(f32[1536,1024]{0,1:T(8,128)} %get-tuple-element.6, f32[1536,1024]{0,1:T(8,128)} %get-tuple-element.5), kind=kLoop, calls=%fused_computation | loop fusion | flops 6291456 | bytes 18874368 | tf_op jit(solution)/shard_map/convert_element_type | solution.py:41
  413.7 0.0 copy-start.2
  413.7 1.7 dynamic-slice_select_fusion.1
  415.4 0.4 copy-done.2
  415.9 1.5 dynamic-slice_select_fusion
  417.4 0.0 all-reduce.7.cloned.1.call-update
  417.4 151.0 %all-reduce.7.cloned.1.call-done = (bf16[768,1024]{0,1:T(8,128)(2,1)}, bf16[768,1024]{0,1:T(8,128)(2,1)}) async-done(((bf16[768,1024]{0,1:T(8,128)(2,1)}, bf16[768,1024]{0,1:T(8,128)(2,1)}), (bf16[768,1024]{0,1:T(8,128)(2,1)}, bf16[768,1024]{0,1:T(8,128)(2,1)})) %all-reduce.7.cloned.1.call-update) | async-done | bytes 3145744 | tf_op jit(solution)/shard_map/psum | solution.py:19
  568.4 0.0 copy-start.3
  568.4 0.0 copy-start.6
  568.4 4.3 fusion.10
  572.7 0.0 copy-done.3
  572.7 0.0 copy-done.6
  572.7 0.0 copy-start.1
  572.7 6.4 %add_add_fusion = f32[1536,768]{1,0:T(8,128)} fusion(f32[1536,768]{1,0:T(8,128)} %param.7, f32[1536,768]{1,0:T(8,128)S(1)} %fusion.10, bf16[1536,1024]{0,1:T(8,128)(2,1)S(1)} %copy-done.3, bf16[768,1024]{0,1:T(8,128)(2,1)S(1)} %copy-done.6), kind=kOutput, calls=%fused_computation.2 | convolution fusion | flops 2418278400 | bytes 18874368 | tf_op jit(solution)/shard_map/dot_general | solution.py:44
  579.1 0.0 copy-done.1
Async XLA Ops:
  6.5 182.5 %copy-start = (bf16[1536,768]{1,0:T(8,128)(2,1)S(1)}, bf16[1536,768]{1,0:T(8,128)(2,1)}, u32[]{:S(2)}) copy-start(bf16[1536,768]{1,0:T(8,128)(2,1)} %param.4) | copy-start | bytes 7077892
  6.5 3.5 copy-start.4
  6.5 3.5 copy-start.5
  6.5 42.6 %reduce-scatter.5.cloned.1.call-start = ((), (), s32[]{:S(2)}) async-start(), calls=%async_computation.4 | async-start | bytes 3932160 | tf_op jit(solution)/shard_map/reduce_scatter | solution.py:13
  10.0 79.6 %reduce-scatter.9.cloned.1.call-start = ((), (), s32[]{:S(2)}) async-start(), calls=%async_computation.7 | async-start | bytes 3932160 | tf_op jit(solution)/shard_map/reduce_scatter | solution.py:13
  12.3 102.6 %reduce-scatter.7.cloned.1.call-start = ((), (), s32[]{:S(2)}) async-start(), calls=%async_computation.5 | async-start | bytes 1179648 | tf_op jit(solution)/shard_map/reduce_scatter | solution.py:13
  49.2 88.8 %reduce-scatter.11.cloned.1.call-start = ((), (), s32[]{:S(2)}) async-start(), calls=%async_computation.8 | async-start | bytes 1179648 | tf_op jit(solution)/shard_map/reduce_scatter | solution.py:13
  89.6 99.4 %all-gather.3.cloned.1.call-start = ((), (), s32[]{:S(2)}) async-start(), calls=%async_computation.6 | async-start | bytes 1769472 | tf_op jit(solution)/shard_map/all_gather | solution.py:37
  116.6 125.6 %all-gather.5.cloned.1.call-start = ((), (), s32[]{:S(2)}) async-start(), calls=%async_computation.9 | async-start | bytes 1769472 | tf_op jit(solution)/shard_map/all_gather | solution.py:37
  139.7 267.7 %all-reduce.5.cloned.1.call-start = ((), (), s32[]{:S(2)}) async-start(), calls=%async_computation.10 | async-start | bytes 25165824 | tf_op jit(solution)/shard_map/psum | solution.py:40
  248.1 320.3 %all-reduce.7.cloned.1.call-start = ((), (), s32[]{:S(2)}) async-start(), calls=%async_computation.11 | async-start | bytes 6291456 | tf_op jit(solution)/shard_map/psum | solution.py:19
  413.7 2.2 copy-start.2
  568.4 4.3 copy-start.3
  568.4 4.3 copy-start.6
  572.7 6.4 %copy-start.1 = (bf16[1536,768]{1,0:T(8,128)(2,1)S(1)}, bf16[1536,768]{1,0:T(8,128)(2,1)}, u32[]{:S(2)}) copy-start(bf16[1536,768]{1,0:T(8,128)(2,1)} %param.4) | copy-start | bytes 7077892
Sparse Core Ops, SparseCore 0:
  10.1 38.9 reduce-scatter.4
  51.6 37.9 reduce-scatter.8
  91.9 22.8 reduce-scatter.6
  117.0 20.8 reduce-scatter.10
  140.0 48.9 all-gather.2
  191.0 51.0 all-gather.4
  248.2 159.1 all-reduce.4
  417.5 150.8 all-reduce.6
where the time goes:
time: 586 us
  waiting for transfers between devices  530 us (90%)
  matrix products  28.4 us (5%)
  between operations  13.6 us (2%)
  other arithmetic  12.9 us (2%)
    psum x1, waiting for transfers between devices, body(): summed = lax.psum(terms, ('sec', 'col'))  159 us
    psum x1, waiting for transfers between devices, from_root(): return lax.psum(jnp.where(mine, x, jnp.zeros_like(x)), axis)  151 us
    reduce_scatter x4, waiting for transfers between devices, scatter_axes(): x = lax.psum_scatter(x, axis, scatter_dimension=dim, tiled=True)  124 us
    all_gather x2, waiting for transfers between devices, body(): lax.all_gather(scaled, ROW, axis=1, tiled=True)  96.2 us
    dot_general x2, matrix products, body(): jnp.dot(held_inverse, lax.all_gather(scaled, ROW, axis=1, tiled=True), pr...  12.1 us
  transfers between devices with their start and end apart: 8, of which 8 were waited for; matrix products, arithmetic and copies ran while one was open for 2% of the time, Pallas kernels for 0%

commit v1 on v0

--- a/solution.py
+++ b/solution.py
@@ -6,6 +6,11 @@
 
 PANELS = 2
 ROW = ("row_0", "row_1")
+
+
+def all_by_exchange(x, axis, d):
+    sent = jnp.stack([x] * lax.axis_size(axis))
+    return jnp.concatenate(lax.all_to_all(sent, axis, 0, 0), axis=d)
 
 
 def scatter_axes(x, axes, dim):
@@ -33,9 +38,7 @@
         )
         scaled = scatter_axes(partial_value, ROW, 1).astype(jnp.bfloat16)
         terms = jnp.dot(
-            held_inverse,
-            lax.all_gather(scaled, ROW, axis=1, tiled=True),
-            preferred_element_type=jnp.float32,
+            held_inverse, all_by_exchange(scaled, ROW, 1), preferred_element_type=jnp.float32
         )
         summed = lax.psum(terms, ("sec", "col"))
         inverse = (-summed).astype(jnp.bfloat16)

time: 586 us -> 524 us (0.89)
  waiting for transfers between devices: 530 us -> 458 us
  starting transfers between devices: 0.29 us -> 9.07 us
    all_gather x2 -> x0, waiting for transfers between devices: 96.2 us -> none  [body(): lax.all_gather(scaled, ROW, axis=1, tiled=True)]
    all_to_all x0 -> x2, waiting for transfers between devices: none -> 16.4 us  [all_by_exchange(): return jnp.concatenate(lax.all_to_all(sent, axis, 0, 0), axis=d)]
    reduce_scatter x4, waiting for transfers between devices: 124 us -> 133 us  [scatter_axes(): x = lax.psum_scatter(x, axis, scatter_dimension=dim, tiled=True)]
    all_to_all x0 -> x2, starting transfers between devices: none -> 8.91 us  [all_by_exchange(): return jnp.concatenate(lax.all_to_all(sent, axis, 0, 0), axis=d)]
  transfers between devices with their start and end apart: 8 -> 8, of which waited for: 8 -> 7; matrix products, arithmetic and copies ran while one was open for 2% -> 2% of each run, Pallas kernels for 0% -> 0%
where the time goes in v1:
time: 524 us
  waiting for transfers between devices  458 us (87%)
  matrix products  28.3 us (5%)
  between operations  13.6 us (3%)
  other arithmetic  11.6 us (2%)
  starting transfers between devices  9.07 us (2%)
    psum x1, waiting for transfers between devices, body(): summed = lax.psum(terms, ('sec', 'col'))  158 us
    psum x1, waiting for transfers between devices, from_root(): return lax.psum(jnp.where(mine, x, jnp.zeros_like(x)), axis)  151 us
    reduce_scatter x4, waiting for transfers between devices, scatter_axes(): x = lax.psum_scatter(x, axis, scatter_dimension=dim, tiled=True)  133 us
    all_to_all x2, waiting for transfers between devices, all_by_exchange(): return jnp.concatenate(lax.all_to_all(sent, axis, 0, 0), axis=d)  16.4 us
    dot_general x2, matrix products, body(): jnp.dot(held_inverse, all_by_exchange(scaled, ROW, 1), preferred_element_...  12 us
    dot_general x2, matrix products, body(): lax.dot_general(inverse, column_block, (((1,), (1,)), ((), ())), preferre...  10.7 us
  transfers between devices with their start and end apart: 8, of which 7 were waited for; matrix products, arithmetic and copies ran while one was open for 2% of the time, Pallas kernels for 0%

profile of v1, /device:TPU:5, one launch (start us, length us, event | category | flops | bytes accessed | tf_op | source)
XLA Modules:
  0.0 523.6 jit_solution(15603161742956009931)
XLA Ops:
  6.5 0.0 copy-start
  6.5 0.0 copy-start.4
  6.5 0.0 copy-start.5
  6.5 0.0 reduce-scatter.5.cloned.1.call-start
  6.5 3.4 fusion.2
  10.0 0.0 reduce-scatter.5.cloned.1.call-update
  10.0 0.0 reduce-scatter.9.cloned.1.call-start
  10.0 0.0 copy-done.4
  10.0 0.0 copy-done.5
  10.1 2.2 fusion
  12.3 0.0 reduce-scatter.9.cloned.1.call-update
  12.3 0.0 reduce-scatter.7.cloned.1.call-start
  12.3 36.8 %reduce-scatter.5.cloned.1.call-done = f32[768,256]{1,0:T(8,128)} async-done(((f32[768,1024]{1,0:T(8,128)}), f32[768,256]{1,0:T(8,128)}) %reduce-scatter.5.cloned.1.call-update) | async-done | bytes 786448 | tf_op jit(solution)/shard_map/reduce_scatter | solution.py:18
  49.2 0.0 reduce-scatter.7.cloned.1.call-update
  49.2 0.0 reduce-scatter.11.cloned.1.call-start
  49.2 40.3 %reduce-scatter.9.cloned.1.call-done = f32[768,256]{1,0:T(8,128)} async-done(((f32[768,1024]{1,0:T(8,128)}), f32[768,256]{1,0:T(8,128)}) %reduce-scatter.9.cloned.1.call-update) | async-done | bytes 786448 | tf_op jit(solution)/shard_map/reduce_scatter | solution.py:18
  89.6 0.0 reduce-scatter.11.cloned.1.call-update
  89.6 25.3 %reduce-scatter.7.cloned.1.call-done = f32[768,128]{1,0:T(8,128)} async-done(((f32[768,256]{1,0:T(8,128)}), f32[768,128]{1,0:T(8,128)}) %reduce-scatter.7.cloned.1.call-update) | async-done | bytes 393232 | tf_op jit(solution)/shard_map/reduce_scatter | solution.py:18
  114.8 1.0 convert_element_type.12
  115.9 0.1 copy.5
  116.0 1.2 stack.4
  117.3 4.4 all-to-all-start
  121.7 30.4 %reduce-scatter.11.cloned.1.call-done = f32[768,128]{1,0:T(8,128)} async-done(((f32[768,256]{1,0:T(8,128)}), f32[768,128]{1,0:T(8,128)}) %reduce-scatter.11.cloned.1.call-update) | async-done | bytes 393232 | tf_op jit(solution)/shard_map/reduce_scatter | solution.py:18
  152.1 1.0 convert_element_type.14
  153.2 0.1 copy.6
  153.3 0.0 all-to-all-done
  153.3 1.2 stack.5
  154.6 4.5 all-to-all-start.1
  159.0 0.0 all-reduce.5.cloned.1.call-start
  159.0 0.0 copy-done
  159.1 6.1 %convolution_bitcast_fusion.1 = f32[1536,1024]{0,1:T(8,128)} fusion(bf16[768,1024]{0,1:T(8,128)(2,1)} %bitcast.3, bf16[1536,768]{1,0:T(8,128)(2,1)S(1)} %copy-done), kind=kOutput, calls=%fused_computation.4 | convolution fusion | flops 2415919104 | bytes 10223616 | tf_op jit(solution)/shard_map/dot_general | solution.py:40
  165.1 16.4 %all-to-all-done.1 = bf16[8,768,128]{1,2,0:T(8,128)(2,1)} async-done(((bf16[8,768,128]{1,2,0:T(8,128)(2,1)}), bf16[8,768,128]{1,2,0:T(8,128)(2,1)}, u32[]{:S(2)}, u32[]{:S(2)}) %all-to-all-start.1) | async-done | bytes 1572896 | tf_op jit(solution)/shard_map/all_to_all | solution.py:13
  181.5 6.0 %convolution_bitcast_fusion = f32[1536,1024]{0,1:T(8,128)} fusion(bf16[768,1024]{0,1:T(8,128)(2,1)} %bitcast.8, bf16[1536,768]{1,0:T(8,128)(2,1)S(1)} %copy-done), kind=kOutput, calls=%fused_computation.3 | convolution fusion | flops 2415919104 | bytes 10223616 | tf_op jit(solution)/shard_map/dot_general | solution.py:40
  187.4 0.0 all-reduce.5.cloned.1.call-update
  187.4 0.0 all-reduce.7.cloned.1.call-start
  187.5 157.5 %all-reduce.5.cloned.1.call-done = (f32[1536,1024]{0,1:T(8,128)}, f32[1536,1024]{0,1:T(8,128)}) async-done(((f32[1536,1024]{0,1:T(8,128)}, f32[1536,1024]{0,1:T(8,128)}), (f32[1536,1024]{0,1:T(8,128)}, f32[1536,1024]{0,1:T(8,128)})) %all-reduce.5.cloned.1.call-update) | async-done | bytes 12582928 | tf_op jit(solution)/shard_map/psum | solution.py:43
  345.1 6.3 %negate_convert_fusion = (bf16[1536,1024]{0,1:T(8,128)(2,1)S(1)}, bf16[1536,1024]{0,1:T(8,128)(2,1)S(1)}) fusion(f32[1536,1024]{0,1:T(8,128)} %get-tuple-element.6, f32[1536,1024]{0,1:T(8,128)} %get-tuple-element.5), kind=kLoop, calls=%fused_computation | loop fusion | flops 6291456 | bytes 18874368 | tf_op jit(solution)/shard_map/convert_element_type | solution.py:44
  351.4 0.0 copy-start.2
  351.4 1.7 dynamic-slice_select_fusion.1
  353.1 0.4 copy-done.2
  353.6 1.5 dynamic-slice_select_fusion
  355.1 0.0 all-reduce.7.cloned.1.call-update
  355.1 151.0 %all-reduce.7.cloned.1.call-done = (bf16[768,1024]{0,1:T(8,128)(2,1)}, bf16[768,1024]{0,1:T(8,128)(2,1)}) async-done(((bf16[768,1024]{0,1:T(8,128)(2,1)}, bf16[768,1024]{0,1:T(8,128)(2,1)}), (bf16[768,1024]{0,1:T(8,128)(2,1)}, bf16[768,1024]{0,1:T(8,128)(2,1)})) %all-reduce.7.cloned.1.call-update) | async-done | bytes 3145744 | tf_op jit(solution)/shard_map/psum | solution.py:24
  506.1 0.0 copy-start.3
  506.1 0.0 copy-start.6
  506.1 4.3 fusion.10
  510.4 0.0 copy-done.3
  510.4 0.0 copy-done.6
  510.4 0.0 copy-start.1
  510.4 6.4 %add_add_fusion = f32[1536,768]{1,0:T(8,128)} fusion(f32[1536,768]{1,0:T(8,128)} %param.7, f32[1536,768]{1,0:T(8,128)S(1)} %fusion.10, bf16[1536,1024]{0,1:T(8,128)(2,1)S(1)} %copy-done.3, bf16[768,1024]{0,1:T(8,128)(2,1)S(1)} %copy-done.6), kind=kOutput, calls=%fused_computation.2 | convolution fusion | flops 2418278400 | bytes 18874368 | tf_op jit(solution)/shard_map/dot_general | solution.py:47
  516.8 0.0 copy-done.1
Async XLA Ops:
  6.5 152.5 %copy-start = (bf16[1536,768]{1,0:T(8,128)(2,1)S(1)}, bf16[1536,768]{1,0:T(8,128)(2,1)}, u32[]{:S(2)}) copy-start(bf16[1536,768]{1,0:T(8,128)(2,1)} %param.4) | copy-start | bytes 7077892
  6.5 3.5 copy-start.4
  6.5 3.5 copy-start.5
  6.5 42.6 %reduce-scatter.5.cloned.1.call-start = ((), (), s32[]{:S(2)}) async-start(), calls=%async_computation.6 | async-start | bytes 3932160 | tf_op jit(solution)/shard_map/reduce_scatter | solution.py:18
  10.0 79.6 %reduce-scatter.9.cloned.1.call-start = ((), (), s32[]{:S(2)}) async-start(), calls=%async_computation.8 | async-start | bytes 3932160 | tf_op jit(solution)/shard_map/reduce_scatter | solution.py:18
  12.3 102.5 %reduce-scatter.7.cloned.1.call-start = ((), (), s32[]{:S(2)}) async-start(), calls=%async_computation.7 | async-start | bytes 1179648 | tf_op jit(solution)/shard_map/reduce_scatter | solution.py:18
  49.2 103.0 %reduce-scatter.11.cloned.1.call-start = ((), (), s32[]{:S(2)}) async-start(), calls=%async_computation.9 | async-start | bytes 1179648 | tf_op jit(solution)/shard_map/reduce_scatter | solution.py:18
  117.3 36.1 %all-to-all-start = ((bf16[8,768,128]{1,2,0:T(8,128)(2,1)}), bf16[8,768,128]{1,2,0:T(8,128)(2,1)}, u32[]{:S(2)}, u32[]{:S(2)}) async-start(bf16[8,768,128]{1,2,0:T(8,128)(2,1)} %stack.4), calls=%async_computation.2 | async-start | bytes 3145728 | tf_op jit(solution)/shard_map/all_to_all | solution.py:13
  154.6 26.9 %all-to-all-start.1 = ((bf16[8,768,128]{1,2,0:T(8,128)(2,1)}), bf16[8,768,128]{1,2,0:T(8,128)(2,1)}, u32[]{:S(2)}, u32[]{:S(2)}) async-start(bf16[8,768,128]{1,2,0:T(8,128)(2,1)} %stack.5), calls=%async_computation.5 | async-start | bytes 3145728 | tf_op jit(solution)/shard_map/all_to_all | solution.py:13
  159.0 186.0 %all-reduce.5.cloned.1.call-start = ((), (), s32[]{:S(2)}) async-start(), calls=%async_computation.10 | async-start | bytes 25165824 | tf_op jit(solution)/shard_map/psum | solution.py:43
  187.4 318.6 %all-reduce.7.cloned.1.call-start = ((), (), s32[]{:S(2)}) async-start(), calls=%async_computation.11 | async-start | bytes 6291456 | tf_op jit(solution)/shard_map/psum | solution.py:24
  351.4 2.2 copy-start.2
  506.1 4.3 copy-start.3
  506.1 4.4 copy-start.6
  510.4 6.4 %copy-start.1 = (bf16[1536,768]{1,0:T(8,128)(2,1)S(1)}, bf16[1536,768]{1,0:T(8,128)(2,1)}, u32[]{:S(2)}) copy-start(bf16[1536,768]{1,0:T(8,128)(2,1)} %param.4) | copy-start | bytes 7077892
Sparse Core Ops, SparseCore 0:
  10.1 38.9 reduce-scatter.4
  51.6 37.9 reduce-scatter.8
  91.9 22.8 reduce-scatter.6
  117.0 35.0 reduce-scatter.10
  187.6 157.4 all-reduce.4
  355.2 150.8 all-reduce.6
